TPU v7x, 32 devices: a whole 2x2x4 slice. The times are simulated.
32 devices in a mesh: rows: 8 (over z, y), cols: 4 (over x, core).
Axes of the slice: x: 2, y: 2, z: 4, core: 2. Of those that a mesh axis runs over, the one named last changes fastest.
Arguments:
- sketch: float32 [32768, 256], P(('rows', 'cols'))
- tiles: bfloat16 [1280, 512, 512], P(('rows', 'cols')), may hold values from -48 to 48
- tile_user: int32 [1280], P(('rows', 'cols')), may hold values from 0 to 7
- tile_item: int32 [1280], P(('rows', 'cols')), may hold values from 0 to 7
- tile_count: int32 [32], P(('rows', 'cols')), may hold values from 5 to 40, as said below
- item_owner: int32 [4, 8], P('cols'), may hold values from 0 to 7, each once within a row
Outputs:
- projected: float32 [8, 4, 256, 512], P('rows', 'cols')
Inputs may be any that keep to these rules, and one draw needn't show every extreme that they name: `tile_count`: live slots of a device are its first slots; some device has all 40 live in every draw.
All inputs are finite; a program needn't handle non-finite values.
Results may differ from a plain program's by a relative error of at most 0.0029.
Values may be sent and summed in bfloat16 or wider, within the bound.
No kernel may reach another device: no remote copies, remote signals or barrier semaphores. Data moves between devices by JAX's collectives and lax.ppermute only.
A program may use at most 192 MiB of HBM per device.

v0:
```python
import functools

import jax
import jax.numpy as jnp
from jax import lax
from jax.experimental import pallas as pl
from jax.experimental.pallas import tpu as pltpu
from jax.sharding import PartitionSpec as P

F32 = jnp.float32
BF16 = jnp.bfloat16
HIGH = lax.Precision.HIGHEST
SLOTS = 12
SPARE = 4 * 2**20
GROUP = 4
NEAR_COST = 200 * 2**20
EARLY_COST = 1024
LATE_COST = 1024
FACTOR_COST = 200 * 2**20
CHUNKS = (160, 96)
NEWTON = 2


def bits_of(count):
    return [1 << b for b in reversed(range(count.bit_length() - 1))]


def swap(x, axis, count, bit):
    return lax.ppermute(x, axis, [(i, i ^ bit) for i in range(count)])


def places(order, parity):
    found = [parity << order[0]]
    for bit in reversed(order[1:]):
        found = found + [p | (1 << bit) for p in found]
    return found


def run_tiles(base, span, per_piece, users, items, owner, meta, tiles, slab, add, buf, sems, order):
    count, row, col = meta[0], meta[1], meta[2]

    def relative(t):
        user = users[t]
        return lax.bitwise_xor(user // per_piece, col) - base, lax.rem(user, per_piece)

    def choose(t, n):
        piece, _ = relative(t)
        order[n] = t
        return n + jnp.where((piece >= 0) & (piece < span), 1, 0)

    live = lax.fori_loop(0, count, choose, 0)

    def fetch(i):
        slot = lax.rem(i, SLOTS)
        return pltpu.make_async_copy(tiles.at[order[i]], buf.at[slot], sems.at[slot])

    for i in range(SLOTS):
        @pl.when(i < live)
        def _():
            fetch(i).start()

    def group(first, size):
        for q in range(size):
            fetch(first + q).wait()
        found = []
        for q in range(size):
            piece, part = relative(order[first + q])
            both = jnp.dot(
                slab[piece * per_piece + part],
                buf[lax.rem(first + q, SLOTS)],
                preferred_element_type=F32,
            )
            found.append(both)
        for q in range(size):
            add(lax.bitwise_xor(owner[items[order[first + q]]], row), found[q])
        for q in range(size):
            @pl.when(first + q + SLOTS < live)
            def _():
                fetch(first + q + SLOTS).start()

    def finish():
        groups = live // GROUP

        def many(g, _):
            group(g * GROUP, GROUP)
            return 0

        def one(i, _):
            group(i, 1)
            return 0

        lax.fori_loop(0, groups, many, 0)
        lax.fori_loop(groups * GROUP, live, one, 0)

    return finish


def split_kernel(sketch, flat, whole, chunk):
    flat[...] = sketch[...].T
    first = 0
    for kc in CHUNKS:
        rows = flat[first : first + kc, :]
        high = rows.astype(BF16)
        low = (rows - high.astype(F32)).astype(BF16)
        for i, part in enumerate((high, low)):
            start = 2 * first + i * kc
            whole[start : start + kc, :] = part
            if first == 0:
                chunk[start : start + kc, :] = part
        first += kc


def split_sketch(sketch):
    users, width = sketch.shape
    vmem = pl.BlockSpec(memory_space=pltpu.VMEM)
    return pl.pallas_call(
        split_kernel,
        out_shape=[jax.ShapeDtypeStruct((width, users), F32)]
        + [jax.ShapeDtypeStruct((k, users), BF16) for k in (2 * width, 2 * CHUNKS[0])],
        in_specs=[vmem],
        out_specs=[vmem] * 3,
        compiler_params=pltpu.CompilerParams(vmem_limit_bytes=16 * 2**20),
    )(sketch)


def gram_kernel(flat, packed):
    n = packed.shape[1]
    top, low = flat[:n, :], flat[n:, :]
    second = mmt(low, low)
    r = lax.broadcasted_iota(jnp.int32, (n, n), 0)
    c = lax.broadcasted_iota(jnp.int32, (n, n), 1)
    packed[:n] = jnp.where(r >= c, mmt(top, top), second)
    packed[n : 2 * n] = mmt(low, top)
    tail = jnp.sum(jnp.where(r == c, second, 0.0), axis=0, keepdims=True)
    packed[2 * n :] = jnp.broadcast_to(tail, (8, n))


def packed_gram(flat):
    n = flat.shape[0] // 2
    vmem = pl.BlockSpec(memory_space=pltpu.VMEM)
    return pl.pallas_call(
        gram_kernel,
        out_shape=jax.ShapeDtypeStruct((2 * n + 8, n), F32),
        in_specs=[vmem],
        out_specs=vmem,
        compiler_params=pltpu.CompilerParams(vmem_limit_bytes=16 * 2**20),
    )(flat)


def fill(slab, pieces, per_piece):
    tile_size = slab.shape[2]
    for c, blocks in enumerate(pieces):
        first = 0
        for block in blocks:
            stop = first + block.shape[0]
            for h in range(per_piece):
                slab[c * per_piece + h, first:stop, :] = block[:, h * tile_size : (h + 1) * tile_size]
            first = stop


def near_kernel(span, users, items, owner, meta, *refs):
    pieces = [refs[i : i + 1] for i in range(span)]
    tiles = refs[span]
    sums = refs[span + 1 : -4]
    slab, buf, sems, order = refs[-4:]
    per_piece = refs[0].shape[1] // tiles.shape[1]

    def add(place, both):
        first = 0
        for part in sums:
            kc = part.shape[1]
            part[place] += both[first : first + kc] + both[first + kc : first + 2 * kc]
            first += 2 * kc

    finish = run_tiles(
        0, span, per_piece, users, items, owner, meta, tiles, slab, add, buf, sems, order
    )
    for part in sums:
        part[...] = jnp.zeros_like(part)
    fill(slab, pieces, per_piece)
    finish()


def far_kernel(span, blocks, orders, users, items, owner, meta, *refs):
    pieces = [refs[i * blocks : (i + 1) * blocks] for i in range(span)]
    start, tiles = refs[span * blocks], refs[span * blocks + 1]
    outs = refs[span * blocks + 2 : -5]
    slab, buf, sems, order, acc = refs[-5:]
    tile_size = tiles.shape[1]
    per_piece = refs[0].shape[1] // tile_size
    kc = start.shape[1]

    def add(place, both):
        acc[place] += both[:kc] + both[kc:]

    finish = run_tiles(
        span, span, per_piece, users, items, owner, meta, tiles, slab, add, buf, sems, order
    )
    acc[...] = start[...]
    fill(slab, pieces, per_piece)
    finish()
    width = tile_size // len(orders)
    for o, bits in enumerate(orders):
        cut = slice(o * width, (o + 1) * width)
        for k, place in enumerate(places(bits, 0)):
            outs[2 * o][k] = acc[place, :, cut]
        for k, place in enumerate(places(bits, 1)):
            outs[2 * o + 1][k] = acc[place, :, cut].astype(BF16)


def tile_call(kernel, scalars, pieces, extra, tiles, shapes, scratch, cost):
    users = scalars[0].shape[0]
    tile_size = tiles.shape[1]
    count = len(pieces) * pieces[0][0].shape[1] // tile_size
    depth = sum(block.shape[0] for block in pieces[0])
    pieces = [block for blocks in pieces for block in blocks]
    smem = pl.BlockSpec(memory_space=pltpu.SMEM)
    vmem = pl.BlockSpec(memory_space=pltpu.VMEM)
    slab = jax.ShapeDtypeStruct((count, depth, tile_size), BF16)
    buf = jax.ShapeDtypeStruct((SLOTS, tile_size, tile_size), BF16)
    held = sum(x.size * x.dtype.itemsize for x in (*pieces, *extra, *shapes, *scratch, slab, buf))
    return pl.pallas_call(
        kernel,
        out_shape=shapes,
        in_specs=[smem] * len(scalars)
        + [vmem] * (len(pieces) + len(extra))
        + [pl.BlockSpec(memory_space=pl.ANY)],
        out_specs=[vmem] * len(shapes),
        scratch_shapes=[
            pltpu.VMEM(slab.shape, BF16),
            pltpu.VMEM(buf.shape, BF16),
            pltpu.SemaphoreType.DMA((SLOTS,)),
            pltpu.SMEM((users,), jnp.int32),
        ]
        + [pltpu.VMEM(x.shape, x.dtype) for x in scratch],
        compiler_params=pltpu.CompilerParams(vmem_limit_bytes=held + SPARE),
        cost_estimate=pl.CostEstimate(flops=0, bytes_accessed=cost, transcendentals=0),
    )(*scalars, *pieces, *extra, tiles)


def near_sums(scalars, pieces, tiles, rows):
    tile_size = tiles.shape[1]
    shapes = [jax.ShapeDtypeStruct((rows, kc, tile_size), F32) for kc in CHUNKS]
    return tile_call(
        functools.partial(near_kernel, len(pieces)), scalars, [[p] for p in pieces], [], tiles, shapes, [], NEAR_COST
    )


def far_sums(scalars, pieces, start, tiles, orders, cost):
    rows, kc, tile_size = start.shape
    width = tile_size // len(orders)
    shapes = []
    for _ in orders:
        shapes.append(jax.ShapeDtypeStruct((rows // 2, kc, width), F32))
        shapes.append(jax.ShapeDtypeStruct((rows // 2, kc, width), BF16))
    return tile_call(
        functools.partial(far_kernel, len(pieces), len(pieces[0]), orders),
        scalars,
        pieces,
        [start],
        tiles,
        shapes,
        [jax.ShapeDtypeStruct(start.shape, F32)],
        cost,
    )


def mm(a, b):
    return lax.dot_general(a, b, (((1,), (0,)), ((), ())), precision=HIGH, preferred_element_type=F32)


def mmt(a, b):
    return lax.dot_general(a, b, (((1,), (1,)), ((), ())), precision=HIGH, preferred_element_type=F32)


def factor_kernel(packed, inverse, good):
    n = packed.shape[1]
    r = lax.broadcasted_iota(jnp.int32, (n, n), 0)
    c = lax.broadcasted_iota(jnp.int32, (n, n), 1)
    mixed = packed[:n]
    flipped = mixed.T
    side = packed[n : 2 * n]
    tail = jnp.broadcast_to(packed[2 * n : 2 * n + 1], (n, n))
    first = jnp.where(r >= c, mixed, flipped)
    second = jnp.where(r < c, mixed, jnp.where(r > c, flipped, tail))
    gram = jnp.concatenate(
        [jnp.concatenate([first, side.T], axis=1), jnp.concatenate([side, second], axis=1)], axis=0
    )
    m = 2 * n
    rr = lax.broadcasted_iota(jnp.int32, (m, m), 0)
    cc = lax.broadcasted_iota(jnp.int32, (m, m), 1)
    on = rr == cc
    eye = jnp.where(on, 1.0, 0.0).astype(F32)
    low = jnp.where(rr > cc, 1.0, jnp.where(on, 0.5, 0.0)).astype(F32)
    diag = jnp.where(on, gram, 0.0)
    scale_row = lax.rsqrt(jnp.sum(diag, axis=0, keepdims=True))
    scale_col = lax.rsqrt(jnp.sum(diag, axis=1, keepdims=True))
    unit = gram * scale_row * scale_col
    off = unit - eye
    square = jnp.dot(off, off, preferred_element_type=F32)
    spread = jnp.max(jnp.sum(jnp.abs(jnp.dot(square, square, preferred_element_type=F32)), axis=1))
    w = eye - low * off
    for _ in range(NEWTON):
        err = mmt(mm(w, unit), w) - eye
        w = w - mm(low * err, w)
    last = jnp.max(jnp.sum(jnp.abs(err), axis=1))
    inflation = jnp.max(jnp.sum(w * w, axis=0))
    inverse[...] = w * scale_row
    good[0] = jnp.where((spread < 0.025) & (last < 0.01) & (inflation < 1.1), 1, 0)


def factor(packed):
    n = packed.shape[1]
    return pl.pallas_call(
        factor_kernel,
        out_shape=[jax.ShapeDtypeStruct((2 * n, 2 * n), F32), jax.ShapeDtypeStruct((1,), jnp.int32)],
        in_specs=[pl.BlockSpec(memory_space=pltpu.VMEM)],
        out_specs=[pl.BlockSpec(memory_space=pltpu.VMEM), pl.BlockSpec(memory_space=pltpu.SMEM)],
        compiler_params=pltpu.CompilerParams(vmem_limit_bytes=24 * 2**20),
        cost_estimate=pl.CostEstimate(
            flops=0, bytes_accessed=FACTOR_COST, transcendentals=0
        ),
    )(packed)


def last_kernel(inverse, early, keep0, keep1, came, out):
    left = keep0[0] + came[0].astype(F32)
    right = keep1[0] + came[1].astype(F32)
    total = jnp.concatenate([early[...], jnp.concatenate([left, right], axis=1)], axis=0)
    w = inverse[...]
    wh, th = w.astype(BF16), total.astype(BF16)
    wl = (w - wh.astype(F32)).astype(BF16)
    tl = (total - th.astype(F32)).astype(BF16)
    small = jnp.dot(wh, tl, preferred_element_type=F32) + jnp.dot(wl, th, preferred_element_type=F32)
    out[...] = jnp.dot(wh, th, preferred_element_type=F32) + small


def last(inverse, early, keeps, came):
    vmem = pl.BlockSpec(memory_space=pltpu.VMEM)
    return pl.pallas_call(
        last_kernel,
        out_shape=jax.ShapeDtypeStruct((inverse.shape[0], early.shape[1]), F32),
        in_specs=[vmem] * 5,
        out_specs=vmem,
        compiler_params=pltpu.CompilerParams(vmem_limit_bytes=16 * 2**20),
    )(inverse, early, *keeps, came)


def full_path(rows, cols, sketch, tiles, tile_user, tile_item, tile_count, item_owner, packed):
    n = packed.shape[1]
    r = lax.broadcasted_iota(jnp.int32, (n, n), 0)
    c = lax.broadcasted_iota(jnp.int32, (n, n), 1)
    mixed, side, tail = packed[:n], packed[n : 2 * n], packed[2 * n : 2 * n + 1]
    first = jnp.where(r >= c, mixed, mixed.T)
    second = jnp.where(r < c, mixed, jnp.where(r > c, mixed.T, tail))
    gram = jnp.block([[first, side.T], [side, second]])
    lower = jnp.linalg.cholesky(gram)
    basis = lax.linalg.triangular_solve(lower, sketch, left_side=False, lower=True, transpose_a=True).astype(BF16)
    have = {0: basis}
    for bit in bits_of(cols):
        for place in list(have):
            have[place | bit] = swap(have[place], "cols", cols, bit)
    slab = jnp.concatenate([have[i] for i in range(cols)], axis=0)
    col = lax.axis_index("cols")
    row = lax.axis_index("rows")
    per_piece = sketch.shape[0] // tiles.shape[2]
    owner = item_owner[0]
    tile_size = tiles.shape[2]

    def step(index, sums):
        user = tile_user[index]
        block = lax.bitwise_xor(user // per_piece, col) * per_piece + user % per_piece
        part_rows = lax.dynamic_slice_in_dim(slab, block * tile_size, tile_size, 0)
        part = lax.dot_general(part_rows, tiles[index], (((0,), (0,)), ((), ())), preferred_element_type=F32)
        place = lax.bitwise_xor(owner[tile_item[index]], row)
        now = lax.dynamic_index_in_dim(sums, place, 0, keepdims=False)
        return lax.dynamic_update_index_in_dim(sums, now + part, place, 0)

    totals = jnp.zeros((owner.shape[0], sketch.shape[1], tile_size), F32)
    totals = lax.fori_loop(0, tile_count[0], step, totals)
    for bit in bits_of(rows):
        totals = totals[:bit] + swap(totals[bit:], "rows", rows, bit)
    return totals[0]


def after(value, *others):
    return lax.optimization_barrier((value, *others))[0]


def exchange(lanes, rows):
    groups = []
    for bit in sorted({lane[2] for lane in lanes}):
        members = [i for i, lane in enumerate(lanes) if lane[2] == bit]
        sent = [lanes[i][1].reshape(-1, lanes[i][1].shape[2]) for i in members]
        groups.append((members, swap(jnp.concatenate(sent, axis=0), "rows", rows, 1 << bit)))
    return groups


def received(lanes, groups):
    got = [None] * len(lanes)
    for members, came in groups:
        first = 0
        for i in members:
            shape = lanes[i][1].shape
            size = shape[0] * shape[1]
            got[i] = came[first : first + size].reshape(shape)
            first += size
    return [lane[0] + g.astype(F32) for lane, g in zip(lanes, got)]


def split(total):
    half = total.shape[0] // 2
    return total[:half], total[half:].astype(BF16)


def body(rows, cols, sketch, tiles, tile_user, tile_item, tile_count, item_owner):
    row_bits = rows.bit_length() - 1
    first_order = tuple(range(row_bits))
    orders = (first_order, (1, 0) + first_order[2:])
    row = lax.axis_index("rows")
    col = lax.axis_index("cols")
    meta = jnp.stack([tile_count[0], row, col]).astype(jnp.int32)
    scalars = (tile_user, tile_item, item_owner[0], meta)
    far_bit, *near_bits = bits_of(cols)

    def spread(piece):
        have = {0: piece}
        for bit in near_bits:
            for place in list(have):
                have[place | bit] = swap(have[place], "cols", cols, bit)
        return [have[i] for i in range(cols // 2)]

    fence = lax.optimization_barrier
    far = far_bit
    flat, whole, chunk = split_sketch(sketch)
    near = spread(whole)
    crossed = [swap(c, "cols", cols, far) for c in (chunk, whole[2 * CHUNKS[0] :])]
    packed = packed_gram(flat)
    for bit in near_bits:
        packed = packed + swap(packed, "cols", cols, bit)
    came = swap(packed, "rows", rows, 1)
    near[0] = after(near[0], packed)
    sums = near_sums(scalars, near, tiles, rows)
    packed, came, *sums = fence((packed, came, *sums))
    packed = packed + came
    came = swap(packed, "rows", rows, 2)
    crossed[0] = after(crossed[0], packed)
    pieces = list(zip(*[spread(c) for c in jnp.split(crossed[0], 2, axis=0)]))
    outs = far_sums(scalars, pieces, sums[0], tiles, orders, EARLY_COST)
    packed, came, *outs = fence((packed, came, *outs))
    packed = packed + came
    came = swap(packed, "rows", rows, 4)
    lanes = [(outs[2 * o], outs[2 * o + 1], order[0]) for o, order in enumerate(orders)]
    groups = exchange(lanes, rows)
    crossed[1] = after(crossed[1], packed)
    later = far_sums(scalars, [[p] for p in spread(crossed[1])], sums[1], tiles, orders, LATE_COST)
    flying = [g[1] for g in groups]
    packed, came, *rest = fence((packed, came, *flying, *later))
    groups = [(g[0], x) for g, x in zip(groups, rest)]
    later = rest[len(groups) :]
    packed = packed + came
    stages = [("cols", far)] + [("rows", 1 << b) for b in range(3, row_bits)]

    totals = received(lanes, groups)
    late = [(later[2 * o], later[2 * o + 1]) for o in range(len(orders))]
    for step in range(1, row_bits + 1):
        lanes = []
        if step < row_bits:
            lanes += [(*split(t), order[step]) for t, order in zip(totals, orders)]
        lanes += [(*pair, order[step - 1]) for pair, order in zip(late, orders)]
        groups = exchange(lanes, rows)
        flying = [g[1] for g in groups]
        if step <= len(stages):
            axis, bit = stages[step - 1]
            came = swap(packed, axis, rows if axis == "rows" else cols, bit)
            if step < len(stages):
                packed, came, *flying = fence((packed, came, *flying))
                packed = packed + came
            else:
                packed = packed + came
                inverse, good = factor(after(packed, *[lane[1] for lane in lanes]))
                inverse, *flying = fence((inverse, *flying))
        groups = [(g[0], x) for g, x in zip(groups, flying)]
        if step < row_bits:
            new = received(lanes, groups)
            totals, new = new[: len(orders)], new[len(orders) :]
            late = [split(t) for t in new]
        if step == row_bits - 1:
            early = jnp.concatenate([t[0] for t in totals], axis=1)
    keeps = [lane[0] for lane in lanes]
    came = groups[0][1].reshape(len(lanes), *lanes[0][1].shape[1:])
    out = lax.cond(
        good[0] > 0,
        lambda: last(inverse, early, keeps, came),
        lambda: full_path(rows, cols, sketch, tiles, tile_user, tile_item, tile_count, item_owner, packed),
    )
    return out[None, None]


def solution(mesh):
    placed = (
        P(("rows", "cols"), None),
        P(("rows", "cols"), None, None),
        P(("rows", "cols")),
        P(("rows", "cols")),
        P(("rows", "cols")),
        P("cols", None),
    )
    return jax.shard_map(
        functools.partial(body, mesh.shape["rows"], mesh.shape["cols"]),
        mesh=mesh,
        in_specs=placed,
        out_specs=P("rows", "cols", None, None),
        check_vma=False,
    )
```

profile of v0, /device:TPU:1, one launch (start us, length us, event | category | flops | bytes accessed | tf_op | source)
XLA Modules:
  0.0 715.1 jit_solution(6353380514421445549)
XLA Ops:
  0.0 1.6 shard_map.66
  1.8 2.7 collective-permute-start.10
  4.5 1.4 shard_map.67
  10.4 4.8 shard_map.68
  15.2 4.4 collective-permute-done.10
  21.8 2.5 collective-permute-start.9
  24.3 4.1 shard_map.69
  30.1 4.5 collective-permute-start.15
  35.6 3.6 shard_map.70
  39.2 5.0 collective-permute-done.13
  48.0 4.1 collective-permute-done.18
  52.1 3.9 shard_map.71
  57.9 2.1 collective-permute-start.24
  60.9 2.1 collective-permute-start.23
  63.0 2.2 collective-permute-done.24
  65.3 4.8 collective-permute-done.23
  70.1 644.2 %conditional.1 = (f32[1,1,256,512]{3,2,1,0:T(8,128)S(1)}) conditional(s32[]{:T(128)} %bitcast.27, (s32[1]{0:T(128)}, f32[264,128]{1,0:T(8,128)S(1)}, f32[1024,256]{1,0:T(8,128)S(1)}, s32[1,8]{1,0:T(1,128)S(1)}, s32[40]{0:T(128)S(1)}, /*index=5*/s32[40]{0:T(128)S(1)}, bf16[40,512,512]{2,1,0:T(8,128)(2,1)}) %tuple.89, (f32[2,96,256]{2,1,0:T(8,128)S(1)}, ...), branch_computations={%region_0.7_spmd, %region_7.8_spmd} | conditional | flops 802537728 | bytes 78131984 | solution.py:492
  70.8 11.7 %cholesky.8 = f32[128,128]{1,0:T(8,128)S(1)} custom-call(f32[128,128]{1,0:T(8,128)S(1)} %cholesky.47), custom_call_target="Cholesky" | custom-call | tf_op jit(solution)/shard_map/cond/branch_0_fun/jit(cholesky)/cholesky | solution.py:357
  82.8 9.8 %custom-call.12 = f32[1,128,128]{1,2,0:T(8,128)S(1)} custom-call(f32[1,128,128]{2,1,0:T(8,128)S(1)} %copy.15), custom_call_target="InvertDiagBlocksLowerTriangular" | custom-call | tf_op jit(solution)/shard_map/cond/branch_0_fun/jit(cholesky)/cholesky | solution.py:357
  93.1 11.7 %cholesky.30 = f32[128,128]{1,0:T(8,128)S(1)} custom-call(f32[128,128]{1,0:T(8,128)S(1)} %convolution_subtract_fusion.1), custom_call_target="Cholesky" | custom-call | tf_op jit(solution)/shard_map/cond/branch_0_fun/jit(cholesky)/cholesky | solution.py:357
  107.1 4.1 while.13
  107.9 1.3 bitcast_dynamic-update-slice_fusion.2
  109.9 1.3 bitcast_dynamic-update-slice_fusion.2
  111.2 19.7 %custom-call.13 = f32[2,128,128]{1,2,0:T(8,128)S(1)} custom-call(f32[2,128,128]{2,1,0:T(8,128)S(1)} %get-tuple-element.267), custom_call_target="InvertDiagBlocksLowerTriangular" | custom-call | tf_op jit(solution)/shard_map/cond/branch_0_fun/triangular_solve | solution.py:358
  133.4 3.3 collective-permute-start
  136.7 7.0 collective-permute-done.1
  143.7 4.0 collective-permute-start.2
  147.7 1.7 collective-permute-done.2
  149.3 3.1 pad_maximum_fusion
  152.4 2.5 broadcast.96
  154.9 135.8 %while.12 = (s32[]{:T(128)}, f32[8,256,512]{2,1,0:T(8,128)}, s32[]{:T(128)}, s32[40]{0:T(128)S(1)}, s32[8]{0:T(128)S(1)}, /*index=5*/s32[]{:T(128)}, s32[40]{0:T...) while((s32[]{:T(128)}, f32[8,256,512]{2,1,0:T(8,128)}, ...), condition=%wide.region_6.6_spmd, body=%wide.region_5.5_spmd.sunk | while | flops 134348832 | bytes 2884192 | solution.py:380
  164.0 2.2 fusion.33
  175.3 2.1 fusion.33
  186.5 2.1 fusion.33
  197.8 2.2 fusion.33
  209.1 2.2 fusion.33
  220.3 2.1 fusion.33
  231.6 2.1 fusion.33
  242.8 2.2 fusion.33
  254.1 2.1 fusion.33
  265.4 2.2 fusion.33
  276.6 2.1 fusion.33
  287.9 2.2 fusion.33
  290.7 1.9 slice.120
  292.6 314.8 %collective-permute-start.3 = (f32[4,256,512]{2,1,0:T(8,128)S(1)}, f32[4,256,512]{2,1,0:T(8,128)S(1)}, u32[]{:S(2)}, u32[]{:S(2)}) collective-permute-start(f32[4,256,512]{2,1,0:T(8,128)S(1)} %slice.120), channel_id=1, source_target_pairs={{0,16},{4,20},{8,24},{12,28},{16,0},{20,4},{24,8},{28,12},{1,17},{... | collective-permute-start | bytes 6291464 | tf_op jit(solution)/shard_map/cond/branch_0_fun/ppermute | solution.py:29
  607.5 68.4 %collective-permute-done.3 = f32[4,256,512]{2,1,0:T(8,128)S(1)} collective-permute-done((f32[4,256,512]{2,1,0:T(8,128)S(1)}, f32[4,256,512]{2,1,0:T(8,128)S(1)}, u32[]{:S(2)}, u32[]{:S(2)}) %collective-permute-start.3) | collective-permute-done | bytes 2097184 | tf_op jit(solution)/shard_map/cond/branch_0_fun/ppermute | solution.py:29
  676.5 23.5 %collective-permute-done.4 = f32[2,256,512]{2,1,0:T(8,128)S(1)} collective-permute-done((f32[2,256,512]{2,1,0:T(8,128)S(1)}, f32[2,256,512]{2,1,0:T(8,128)S(1)}, u32[]{:S(2)}, u32[]{:S(2)}) %collective-permute-start.4) | collective-permute-done | bytes 1048608 | tf_op jit(solution)/shard_map/cond/branch_0_fun/ppermute | solution.py:29
  700.3 13.7 %collective-permute-done.5 = f32[1,256,512]{2,1,0:T(8,128)S(1)} collective-permute-done((f32[1,256,512]{2,1,0:T(8,128)S(1)}, f32[1,256,512]{2,1,0:T(8,128)S(1)}, u32[]{:S(2)}, u32[]{:S(2)}) %collective-permute-start.5) | collective-permute-done | bytes 524320 | tf_op jit(solution)/shard_map/cond/branch_0_fun/ppermute | solution.py:29
  (164 shorter events, 59.0 us)
Async XLA Ops:
  1.7 8.7 %collective-permute-start.8 = (bf16[512,1024]{1,0:T(8,128)(2,1)S(1)}, bf16[512,1024]{1,0:T(8,128)(2,1)S(1)}, u32[]{:S(2)}, u32[]{:S(2)}) collective-permute-start(bf16[512,1024]{1,0:T(8,128)(2,1)S(1)} %get-tuple-element.221.refs_0_), channel_id=1, source_target_pairs={{0,1},{1,0},{2,3},{3,2},{4,5},{5,4},{6,7},{7,6},{8,9},{9,8},{10,11... | collective-permute-start | bytes 3145736 | tf_op jit(solution)/shard_map/ppermute | solution.py:29
  1.8 17.8 %collective-permute-start.10 = (bf16[320,1024]{1,0:T(8,128)(2,1)S(1)}, bf16[320,1024]{1,0:T(8,128)(2,1)}, u32[]{:S(2)}, u32[]{:S(2)}) collective-permute-start(bf16[320,1024]{1,0:T(8,128)(2,1)S(1)} %get-tuple-element.226), channel_id=1, source_target_pairs={{0,2},{1,3},{2,0},{3,1},{4,6},{5,7},{6,4},{7,5},{8,10},{9,11},{10,... | collective-permute-start | bytes 1966088 | tf_op jit(solution)/shard_map/ppermute | solution.py:29
  5.9 1.4 collective-permute-start.6
  7.3 7.9 %collective-permute-start.7 = (f32[264,128]{1,0:T(8,128)S(1)}, f32[264,128]{1,0:T(8,128)S(1)}, u32[]{:S(2)}, u32[]{:S(2)}) collective-permute-start(f32[264,128]{1,0:T(8,128)S(1)} %add.134), channel_id=1, source_target_pairs={{0,4},{4,0},{8,12},{12,8},{16,20},{20,16},{24,28},{28,24},{1,5},{5... | collective-permute-start | bytes 405512 | tf_op jit(solution)/shard_map/ppermute | solution.py:29
  9.4 19.0 %collective-permute-start.16 = (bf16[192,1024]{1,0:T(8,128)(2,1)}, bf16[192,1024]{1,0:T(8,128)(2,1)S(1)}, u32[]{:S(2)}, u32[]{:S(2)}) collective-permute-start(bf16[192,1024]{1,0:T(8,128)(2,1)} %slice.148), channel_id=1, source_target_pairs={{0,2},{1,3},{2,0},{3,1},{4,6},{5,7},{6,4},{7,5},{8,10},{9,11},{10,... | collective-permute-start | bytes 1179656 | tf_op jit(solution)/shard_map/ppermute | solution.py:29
  10.4 13.9 %copy-start.3 = (s32[1,8]{1,0:T(1,128)S(1)}, s32[1,8]{1,0:T(1,128)}, u32[]{:S(2)}) copy-start(s32[1,8]{1,0:T(1,128)} %param.15) | copy-start | bytes 100
  10.4 13.9 %copy-start.4 = (s32[40]{0:T(128)S(1)}, s32[40]{0:T(128)}, u32[]{:S(2)}) copy-start(s32[40]{0:T(128)} %items.5) | copy-start | bytes 484
  10.4 13.9 %copy-start.5 = (s32[40]{0:T(128)S(1)}, s32[40]{0:T(128)}, u32[]{:S(2)}) copy-start(s32[40]{0:T(128)} %users.5) | copy-start | bytes 484
  20.7 3.6 collective-permute-start.12
  21.7 2.6 collective-permute-start.11
  21.8 6.6 collective-permute-start.9
  28.4 7.2 %collective-permute-start.17 = (bf16[192,1024]{1,0:T(8,128)(2,1)S(1)}, bf16[192,1024]{1,0:T(8,128)(2,1)S(1)}, u32[]{:S(2)}, u32[]{:S(2)}) collective-permute-start(bf16[192,1024]{1,0:T(8,128)(2,1)S(1)} %collective-permute-done.16.refs_0_), channel_id=1, source_target_pairs={{0,1},{1,0},{2,3},{3,2},{4,5},{5,4},{6,7},{7,6},{8,9},{9,8},{10,11... | collective-permute-start | bytes 1179656 | tf_op jit(solution)/shard_map/ppermute | solution.py:29
  29.2 14.9 %collective-permute-start.14 = (bf16[640,256]{1,0:T(8,128)(2,1)S(1)}, bf16[640,256]{1,0:T(8,128)(2,1)S(1)}, u32[]{:S(2)}, u32[]{:S(2)}) collective-permute-start(bf16[640,256]{1,0:T(8,128)(2,1)S(1)} %bitcast.125), channel_id=1, source_target_pairs={{0,4},{4,0},{8,12},{12,8},{16,20},{20,16},{24,28},{28,24},{1,5},{5... | collective-permute-start | bytes 983048 | tf_op jit(solution)/shard_map/ppermute | solution.py:29
  30.1 15.2 %collective-permute-start.15 = (bf16[640,256]{1,0:T(8,128)(2,1)S(1)}, bf16[640,256]{1,0:T(8,128)(2,1)S(1)}, u32[]{:S(2)}, u32[]{:S(2)}) collective-permute-start(bf16[640,256]{1,0:T(8,128)(2,1)S(1)} %bitcast.124), channel_id=1, source_target_pairs={{0,8},{4,12},{8,0},{12,4},{16,24},{20,28},{24,16},{28,20},{1,9},{5... | collective-permute-start | bytes 983048 | tf_op jit(solution)/shard_map/ppermute | solution.py:29
  34.5 9.6 %collective-permute-start.13 = (f32[264,128]{1,0:T(8,128)S(1)}, f32[264,128]{1,0:T(8,128)S(1)}, u32[]{:S(2)}, u32[]{:S(2)}) collective-permute-start(f32[264,128]{1,0:T(8,128)S(1)} %add.136), channel_id=1, source_target_pairs={{0,16},{4,20},{8,24},{12,28},{16,0},{20,4},{24,8},{28,12},{1,17},{... | collective-permute-start | bytes 405512 | tf_op jit(solution)/shard_map/ppermute | solution.py:29
  45.5 11.1 %collective-permute-start.19 = (bf16[704,256]{1,0:T(8,128)(2,1)S(1)}, bf16[704,256]{1,0:T(8,128)(2,1)S(1)}, u32[]{:S(2)}, u32[]{:S(2)}) collective-permute-start(bf16[704,256]{1,0:T(8,128)(2,1)S(1)} %pad_maximum_fusion.2), channel_id=1, source_target_pairs={{0,4},{4,0},{8,12},{12,8},{16,20},{20,16},{24,28},{28,24},{1,5},{5... | collective-permute-start | bytes 1081352 | tf_op jit(solution)/shard_map/ppermute | solution.py:29
  46.6 10.1 %collective-permute-start.20 = (bf16[704,256]{1,0:T(8,128)(2,1)S(1)}, bf16[704,256]{1,0:T(8,128)(2,1)S(1)}, u32[]{:S(2)}, u32[]{:S(2)}) collective-permute-start(bf16[704,256]{1,0:T(8,128)(2,1)S(1)} %pad_maximum_fusion.3), channel_id=1, source_target_pairs={{0,8},{4,12},{8,0},{12,4},{16,24},{20,28},{24,16},{28,20},{1,9},{5... | collective-permute-start | bytes 1081352 | tf_op jit(solution)/shard_map/ppermute | solution.py:29
  47.9 4.2 collective-permute-start.18
  56.7 13.4 %copy-start.1 = (f32[1024,256]{1,0:T(8,128)S(1)}, f32[1024,256]{1,0:T(8,128)}, u32[]{:S(2)}) copy-start(f32[1024,256]{1,0:T(8,128)} %sketch.1) | copy-start | bytes 3145732
  56.9 3.5 collective-permute-start.21
  57.3 3.5 collective-permute-start.22
  57.9 7.3 %collective-permute-start.24 = (bf16[320,256]{1,0:T(8,128)(2,1)S(1)}, bf16[320,256]{1,0:T(8,128)(2,1)S(1)}, u32[]{:S(2)}, u32[]{:S(2)}) collective-permute-start(bf16[320,256]{1,0:T(8,128)(2,1)S(1)} %pad_maximum_fusion.5), channel_id=1, source_target_pairs={{0,16},{4,20},{8,24},{12,28},{16,0},{20,4},{24,8},{28,12},{1,17},{... | collective-permute-start | bytes 491528 | tf_op jit(solution)/shard_map/ppermute | solution.py:29
  60.9 9.2 %collective-permute-start.23 = (bf16[192,256]{1,0:T(8,128)(2,1)S(1)}, bf16[192,256]{1,0:T(8,128)(2,1)S(1)}, u32[]{:S(2)}, u32[]{:S(2)}) collective-permute-start(bf16[192,256]{1,0:T(8,128)(2,1)S(1)} %pad_maximum_fusion.6), channel_id=1, source_target_pairs={{0,16},{4,20},{8,24},{12,28},{16,0},{20,4},{24,8},{28,12},{1,17},{... | collective-permute-start | bytes 294920 | tf_op jit(solution)/shard_map/ppermute | solution.py:29
  133.3 10.4 %collective-permute-start.1 = (bf16[1024,256]{0,1:T(8,128)(2,1)S(1)}, bf16[1024,256]{0,1:T(8,128)(2,1)S(1)}, u32[]{:S(2)}, u32[]{:S(2)}) collective-permute-start(bf16[1024,256]{0,1:T(8,128)(2,1)S(1)} %pad_maximum_fusion.1), channel_id=1, source_target_pairs={{0,2},{1,3},{2,0},{3,1},{4,6},{5,7},{6,4},{7,5},{8,10},{9,11},{10,... | collective-permute-start | bytes 1572872 | tf_op jit(solution)/shard_map/cond/branch_0_fun/ppermute | solution.py:29
  133.4 14.2 %collective-permute-start = (bf16[1024,256]{0,1:T(8,128)(2,1)S(1)}, bf16[1024,256]{0,1:T(8,128)(2,1)}, u32[]{:S(2)}, u32[]{:S(2)}) collective-permute-start(bf16[1024,256]{0,1:T(8,128)(2,1)S(1)} %pad_maximum_fusion.1), channel_id=1, source_target_pairs={{0,1},{1,0},{2,3},{3,2},{4,5},{5,4},{6,7},{7,6},{8,9},{9,8},{10,11... | collective-permute-start | bytes 1572872 | tf_op jit(solution)/shard_map/cond/branch_0_fun/ppermute | solution.py:29
  143.7 5.7 collective-permute-start.2
  290.7 385.1 %copy-start = (f32[8,256,512]{2,1,0:T(8,128)S(1)}, f32[8,256,512]{2,1,0:T(8,128)}, u32[]{:S(2)}) copy-start(f32[8,256,512]{2,1,0:T(8,128)} %get-tuple-element.173) | copy-start | bytes 12582916 | tf_op jit(solution)/shard_map/cond
  292.6 383.2 %collective-permute-start.3 = (f32[4,256,512]{2,1,0:T(8,128)S(1)}, f32[4,256,512]{2,1,0:T(8,128)S(1)}, u32[]{:S(2)}, u32[]{:S(2)}) collective-permute-start(f32[4,256,512]{2,1,0:T(8,128)S(1)} %slice.120), channel_id=1, source_target_pairs={{0,16},{4,20},{8,24},{12,28},{16,0},{20,4},{24,8},{28,12},{1,17},{... | collective-permute-start | bytes 6291464 | tf_op jit(solution)/shard_map/cond/branch_0_fun/ppermute | solution.py:29
  676.4 23.6 %collective-permute-start.4 = (f32[2,256,512]{2,1,0:T(8,128)S(1)}, f32[2,256,512]{2,1,0:T(8,128)S(1)}, u32[]{:S(2)}, u32[]{:S(2)}) collective-permute-start(f32[2,256,512]{2,1,0:T(8,128)S(1)} %slice.182), channel_id=1, source_target_pairs={{0,8},{4,12},{8,0},{12,4},{16,24},{20,28},{24,16},{28,20},{1,9},{5... | collective-permute-start | bytes 3145736 | tf_op jit(solution)/shard_map/cond/branch_0_fun/ppermute | solution.py:29
  700.3 13.7 %collective-permute-start.5 = (f32[1,256,512]{2,1,0:T(8,128)S(1)}, f32[1,256,512]{2,1,0:T(8,128)S(1)}, u32[]{:S(2)}, u32[]{:S(2)}) collective-permute-start(f32[1,256,512]{2,1,0:T(8,128)S(1)} %slice.184), channel_id=1, source_target_pairs={{0,4},{4,0},{8,12},{12,8},{16,20},{20,16},{24,28},{28,24},{1,5},{5... | collective-permute-start | bytes 1572872 | tf_op jit(solution)/shard_map/cond/branch_0_fun/ppermute | solution.py:29
  714.4 0.8 copy-start.2
where the time goes:
time: 705 us; the launch traced here: 715 us
  starting transfers between devices  345 us (49%)
  waiting for transfers between devices  138 us (20%)
  loops' own time  75.6 us (11%)
  other arithmetic  58.6 us (8%)
  local copies, waits for them, and re-layouts  48.4 us (7%)
  matrix products  28.5 us (4%)
  Pallas kernels  19.4 us (3%)
    ppermute x25, starting transfers between devices, swap(): return lax.ppermute(x, axis, [(i, i ^ bit) for i in range(count)])  345 us
    ppermute x25, waiting for transfers between devices, swap(): return lax.ppermute(x, axis, [(i, i ^ bit) for i in range(count)])  138 us
    another operation x1, loops' own time, full_path(): totals = lax.fori_loop(0, tile_count[0], step, totals)  73.6 us
    another operation x6, other arithmetic, full_path(): lower = jnp.linalg.cholesky(gram)  34.2 us
    dot_general x12, matrix products, step(): lax.dot_general(part_rows, tiles[index], (((0,), (0,)), ((), ())), prefer...  25.8 us
    another operation x5, other arithmetic, full_path(): lax.linalg.triangular_solve(lower, sketch, left_side=False, lower=True, t...  19.8 us
    dynamic_slice x24, local copies, waits for them, and re-layouts, step(): place = lax.bitwise_xor(owner[tile_item[index]], row)  15.5 us
  transfers between devices with their start and end apart: 25, of which 14 were waited for; matrix products, arithmetic and copies ran while one was open for 0% of the time, Pallas kernels for 2%

commit v1 on v0

--- a/solution.py
+++ b/solution.py
@@ -95,18 +95,15 @@
     return finish
 
 
-def split_kernel(sketch, flat, whole, chunk):
+def split_kernel(sketch, flat, *chunks):
     flat[...] = sketch[...].T
     first = 0
-    for kc in CHUNKS:
+    for chunk in chunks:
+        kc = chunk.shape[0] // 2
         rows = flat[first : first + kc, :]
         high = rows.astype(BF16)
-        low = (rows - high.astype(F32)).astype(BF16)
-        for i, part in enumerate((high, low)):
-            start = 2 * first + i * kc
-            whole[start : start + kc, :] = part
-            if first == 0:
-                chunk[start : start + kc, :] = part
+        chunk[:kc, :] = high
+        chunk[kc:, :] = (rows - high.astype(F32)).astype(BF16)
         first += kc
 
 
@@ -116,9 +113,9 @@
     return pl.pallas_call(
         split_kernel,
         out_shape=[jax.ShapeDtypeStruct((width, users), F32)]
-        + [jax.ShapeDtypeStruct((k, users), BF16) for k in (2 * width, 2 * CHUNKS[0])],
+        + [jax.ShapeDtypeStruct((2 * k, users), BF16) for k in CHUNKS],
         in_specs=[vmem],
-        out_specs=[vmem] * 3,
+        out_specs=[vmem] * (1 + len(CHUNKS)),
         compiler_params=pltpu.CompilerParams(vmem_limit_bytes=16 * 2**20),
     )(sketch)
 
@@ -158,10 +155,10 @@
             first = stop
 
 
-def near_kernel(span, users, items, owner, meta, *refs):
-    pieces = [refs[i : i + 1] for i in range(span)]
-    tiles = refs[span]
-    sums = refs[span + 1 : -4]
+def near_kernel(span, blocks, users, items, owner, meta, *refs):
+    pieces = [refs[i * blocks : (i + 1) * blocks] for i in range(span)]
+    tiles = refs[span * blocks]
+    sums = refs[span * blocks + 1 : -4]
     slab, buf, sems, order = refs[-4:]
     per_piece = refs[0].shape[1] // tiles.shape[1]
 
@@ -242,7 +239,7 @@
     tile_size = tiles.shape[1]
     shapes = [jax.ShapeDtypeStruct((rows, kc, tile_size), F32) for kc in CHUNKS]
     return tile_call(
-        functools.partial(near_kernel, len(pieces)), scalars, [[p] for p in pieces], [], tiles, shapes, [], NEAR_COST
+        functools.partial(near_kernel, len(pieces), len(pieces[0])), scalars, pieces, [], tiles, shapes, [], NEAR_COST
     )
 
 
@@ -432,24 +429,23 @@
 
     fence = lax.optimization_barrier
     far = far_bit
-    flat, whole, chunk = split_sketch(sketch)
-    near = spread(whole)
-    crossed = [swap(c, "cols", cols, far) for c in (chunk, whole[2 * CHUNKS[0] :])]
+    flat, *chunks = split_sketch(sketch)
+    near = list(zip(*[spread(c) for c in chunks]))
+    crossed = [swap(c, "cols", cols, far) for c in chunks]
     packed = packed_gram(flat)
     for bit in near_bits:
         packed = packed + swap(packed, "cols", cols, bit)
-    came = swap(packed, "rows", rows, 1)
-    near[0] = after(near[0], packed)
+    came = swap(packed, "rows", rows, 2)
+    near[0] = (after(near[0][0], packed), *near[0][1:])
     sums = near_sums(scalars, near, tiles, rows)
     packed, came, *sums = fence((packed, came, *sums))
     packed = packed + came
-    came = swap(packed, "rows", rows, 2)
+    came = swap(packed, "rows", rows, 4)
     crossed[0] = after(crossed[0], packed)
-    pieces = list(zip(*[spread(c) for c in jnp.split(crossed[0], 2, axis=0)]))
-    outs = far_sums(scalars, pieces, sums[0], tiles, orders, EARLY_COST)
+    outs = far_sums(scalars, [[p] for p in spread(crossed[0])], sums[0], tiles, orders, EARLY_COST)
     packed, came, *outs = fence((packed, came, *outs))
     packed = packed + came
-    came = swap(packed, "rows", rows, 4)
+    came = swap(packed, "cols", cols, far)
     lanes = [(outs[2 * o], outs[2 * o + 1], order[0]) for o, order in enumerate(orders)]
     groups = exchange(lanes, rows)
     crossed[1] = after(crossed[1], packed)
@@ -459,7 +455,7 @@
     groups = [(g[0], x) for g, x in zip(groups, rest)]
     later = rest[len(groups) :]
     packed = packed + came
-    stages = [("cols", far)] + [("rows", 1 << b) for b in range(3, row_bits)]
+    stages = [1] + [1 << b for b in range(3, row_bits)]
 
     totals = received(lanes, groups)
     late = [(later[2 * o], later[2 * o + 1]) for o in range(len(orders))]
@@ -471,15 +467,12 @@
         groups = exchange(lanes, rows)
         flying = [g[1] for g in groups]
         if step <= len(stages):
-            axis, bit = stages[step - 1]
-            came = swap(packed, axis, rows if axis == "rows" else cols, bit)
-            if step < len(stages):
-                packed, came, *flying = fence((packed, came, *flying))
-                packed = packed + came
-            else:
-                packed = packed + came
-                inverse, good = factor(after(packed, *[lane[1] for lane in lanes]))
-                inverse, *flying = fence((inverse, *flying))
+            came = swap(packed, "rows", rows, stages[step - 1])
+            packed, came, *flying = fence((packed, came, *flying))
+            packed = packed + came
+        if step == len(stages) + 1:
+            inverse, good = factor(after(packed, *[lane[1] for lane in lanes]))
+            inverse, *flying = fence((inverse, *flying))
         groups = [(g[0], x) for g, x in zip(groups, flying)]
         if step < row_bits:
             new = received(lanes, groups)

time: 705 us -> 682 us (0.967)
  the two profiles are of different devices: /device:TPU:1 before, /device:TPU:0 now
where the time goes in v1:
time: 682 us; the launch traced here: 669 us
  loops' own time  238 us (35%)
  local copies, waits for them, and re-layouts  125 us (18%)
  waiting for transfers between devices  103 us (15%)
  matrix products  88.9 us (13%)
  other arithmetic  58.5 us (9%)
  Pallas kernels  30.8 us (5%)
  starting transfers between devices  23.5 us (3%)
    another operation x1, loops' own time, full_path(): totals = lax.fori_loop(0, tile_count[0], step, totals)  236 us
    ppermute x25, waiting for transfers between devices, swap(): return lax.ppermute(x, axis, [(i, i ^ bit) for i in range(count)])  103 us
    dot_general x40, matrix products, step(): lax.dot_general(part_rows, tiles[index], (((0,), (0,)), ((), ())), prefer...  86.2 us
    dynamic_slice x80, local copies, waits for them, and re-layouts, step(): place = lax.bitwise_xor(owner[tile_item[index]], row)  46.9 us
    dynamic_slice x40, local copies, waits for them, and re-layouts, step(): now = lax.dynamic_index_in_dim(sums, place, 0, keepdims=False)  43.3 us
    another operation x6, other arithmetic, full_path(): lower = jnp.linalg.cholesky(gram)  34.1 us
    pallas_call x3, Pallas kernels, tile_call(): pl.pallas_call(kernel, out_shape=shapes, in_specs=[smem] * len(scalars) +...  24 us
    dynamic_slice x40, local copies, waits for them, and re-layouts, step(): user = tile_user[index]  23.5 us
  transfers between devices with their start and end apart: 25, of which 10 were waited for; matrix products, arithmetic and copies ran while one was open for 0% of the time, Pallas kernels for 4%

profile of v1, /device:TPU:0, one launch (start us, length us, event | category | flops | bytes accessed | tf_op | source)
XLA Modules:
  0.0 669.3 jit_solution(16714555876716299494)
XLA Ops:
  2.1 2.6 collective-permute-start.11
  10.1 8.6 %shard_map.68 = (f32[8,160,512]{2,1,0:T(8,128)S(1)}, f32[8,96,512]{2,1,0:T(8,128)S(1)}) custom-call(s32[40]{0:T(128)} %users.5, s32[40]{0:T(128)} %items.5, s32[8]{0:T(128)} %bitcast.136, s32[3]{0:T(128)S(1)} %pad_add_fusion.meta, bf16[320,1024]{1,0:T(8,128)(2,1)S(1)} %get-tuple-element.226.refs_0_, bf16[192,1024]{1,0:T(8,128)(2,1)S(1)} %get-tuple-element.227.refs_1_, ...), custom_call_target="tpu_custom_call" | custom-call | bytes 209715200 | tf_op jit(solution)/shard_map/pallas_call | solution.py:219
  21.8 2.6 collective-permute-start.10
  24.4 8.3 %shard_map.69 = (f32[4,160,256]{2,1,0:T(8,128)S(1)}, bf16[4,160,256]{2,1,0:T(8,128)(2,1)S(1)}, f32[4,160,256]{2,1,0:T(8,128)S(1)}, bf16[4,160,256]{2,1,0:T(8,128)(2,1)S(1)}) custom-call(s32[40]{0:T(128)S(1)} %copy-done.6, s32[40]{0:T(128)S(1)} %copy-done.5, s32[8]{0:T(128)S(1)} %bitcast.137, s32[3]{0:T(128)S(1)} %pad_add_fusion.meta, ...), custom_call_target="tpu_custom_call" | custom-call | bytes 1024 | tf_op jit(solution)/shard_map/pallas_call | solution.py:219
  33.3 2.2 collective-permute-start.15
  36.4 7.1 %shard_map.70 = (f32[4,96,256]{2,1,0:T(8,128)S(1)}, bf16[4,96,256]{2,1,0:T(8,128)(2,1)S(1)}, f32[4,96,256]{2,1,0:T(8,128)S(1)}, bf16[4,96,256]{2,1,0:T(8,128)(2,1)S(1)}) custom-call(s32[40]{0:T(128)S(1)} %copy-done.6, s32[40]{0:T(128)S(1)} %copy-done.5, s32[8]{0:T(128)S(1)} %bitcast.138, s32[3]{0:T(128)S(1)} %pad_add_fusion.meta, ...), custom_call_target="tpu_custom_call" | custom-call | bytes 1024 | tf_op jit(solution)/shard_map/pallas_call | solution.py:219
  47.5 8.7 %collective-permute-done.18 = f32[264,128]{1,0:T(8,128)S(1)} collective-permute-done((f32[264,128]{1,0:T(8,128)S(1)}, f32[264,128]{1,0:T(8,128)S(1)}, u32[]{:S(2)}, u32[]{:S(2)}) %collective-permute-start.18) | collective-permute-done | bytes 135200 | tf_op jit(solution)/shard_map/ppermute | solution.py:29
  61.5 3.8 shard_map.71
  67.4 6.1 collective-permute-done.24
  73.5 594.9 %conditional.1 = (f32[1,1,256,512]{3,2,1,0:T(8,128)S(1)}) conditional(s32[]{:T(128)} %bitcast.35, (s32[1]{0:T(128)}, f32[264,128]{1,0:T(8,128)S(1)}, f32[1024,256]{1,0:T(8,128)S(1)}, s32[1,8]{1,0:T(1,128)S(1)}, s32[40]{0:T(128)S(1)}, /*index=5*/s32[40]{0:T(128)S(1)}, bf16[40,512,512]{2,1,0:T(8,128)(2,1)}) %tuple.90, (f32[2,96,256]{2,1,0:T(8,128)S(1)}, ...), branch_computations={%region_0.7_spmd, %region_7.8_spmd} | conditional | flops 802537728 | bytes 80229168 | solution.py:485
  74.2 11.7 %cholesky.8 = f32[128,128]{1,0:T(8,128)S(1)} custom-call(f32[128,128]{1,0:T(8,128)S(1)} %cholesky.47), custom_call_target="Cholesky" | custom-call | tf_op jit(solution)/shard_map/cond/branch_0_fun/jit(cholesky)/cholesky | solution.py:354
  86.2 9.8 %custom-call.12 = f32[1,128,128]{1,2,0:T(8,128)S(1)} custom-call(f32[1,128,128]{2,1,0:T(8,128)S(1)} %copy.15), custom_call_target="InvertDiagBlocksLowerTriangular" | custom-call | tf_op jit(solution)/shard_map/cond/branch_0_fun/jit(cholesky)/cholesky | solution.py:354
  96.6 11.7 %cholesky.30 = f32[128,128]{1,0:T(8,128)S(1)} custom-call(f32[128,128]{1,0:T(8,128)S(1)} %convolution_subtract_fusion.1), custom_call_target="Cholesky" | custom-call | tf_op jit(solution)/shard_map/cond/branch_0_fun/jit(cholesky)/cholesky | solution.py:354
  110.5 3.9 while.13
  114.4 19.7 %custom-call.13 = f32[2,128,128]{1,2,0:T(8,128)S(1)} custom-call(f32[2,128,128]{2,1,0:T(8,128)S(1)} %get-tuple-element.277), custom_call_target="InvertDiagBlocksLowerTriangular" | custom-call | tf_op jit(solution)/shard_map/cond/branch_0_fun/triangular_solve | solution.py:355
  137.3 12.1 %collective-permute-done.1 = bf16[1024,256]{0,1:T(8,128)(2,1)S(1)} collective-permute-done((bf16[1024,256]{0,1:T(8,128)(2,1)S(1)}, bf16[1024,256]{0,1:T(8,128)(2,1)S(1)}, u32[]{:S(2)}, u32[]{:S(2)}) %collective-permute-start.1) | collective-permute-done | bytes 524320 | tf_op jit(solution)/shard_map/cond/branch_0_fun/ppermute | solution.py:29
  151.5 3.1 pad_maximum_fusion
  154.5 2.5 broadcast.96
  157.0 436.3 %while.12 = (s32[]{:T(128)}, f32[8,256,512]{2,1,0:T(8,128)}, s32[]{:T(128)}, s32[40]{0:T(128)S(1)}, s32[8]{0:T(128)S(1)}, /*index=5*/s32[]{:T(128)}, s32[40]{0:T...) while((s32[]{:T(128)}, f32[8,256,512]{2,1,0:T(8,128)}, ...), condition=%wide.region_6.6_spmd, body=%wide.region_5.5_spmd.sunk | while | flops 134348832 | bytes 2884192 | solution.py:377
  165.8 2.2 fusion.30
  176.7 2.2 fusion.30
  187.6 2.2 fusion.30
  209.3 2.2 fusion.30
  231.1 2.2 fusion.30
  252.9 2.2 fusion.30
  263.8 2.2 fusion.30
  285.6 2.2 fusion.30
  296.4 2.2 fusion.30
  307.3 2.2 fusion.30
  350.9 2.2 fusion.30
  361.8 2.2 fusion.30
  372.7 2.2 fusion.30
  383.6 2.2 fusion.30
  405.4 2.2 fusion.30
  416.3 2.2 fusion.30
  427.2 2.2 fusion.30
  438.0 2.2 fusion.30
  448.9 2.2 fusion.30
  459.8 2.2 fusion.30
  470.7 2.2 fusion.30
  481.6 2.2 fusion.30
  536.1 2.2 fusion.30
  547.0 2.2 fusion.30
  557.8 2.2 fusion.30
  590.5 2.2 fusion.30
  595.3 47.9 %collective-permute-done.3 = f32[4,256,512]{2,1,0:T(8,128)S(1)} collective-permute-done((f32[4,256,512]{2,1,0:T(8,128)S(1)}, f32[4,256,512]{2,1,0:T(8,128)S(1)}, u32[]{:S(2)}, u32[]{:S(2)}) %collective-permute-start.3) | collective-permute-done | bytes 2097184 | tf_op jit(solution)/shard_map/cond/branch_0_fun/ppermute | solution.py:29
  643.8 14.8 %collective-permute-done.4 = f32[2,256,512]{2,1,0:T(8,128)S(1)} collective-permute-done((f32[2,256,512]{2,1,0:T(8,128)S(1)}, f32[2,256,512]{2,1,0:T(8,128)S(1)}, u32[]{:S(2)}, u32[]{:S(2)}) %collective-permute-start.4) | collective-permute-done | bytes 1048608 | tf_op jit(solution)/shard_map/cond/branch_0_fun/ppermute | solution.py:29
  658.9 9.2 %collective-permute-done.5 = f32[1,256,512]{2,1,0:T(8,128)S(1)} collective-permute-done((f32[1,256,512]{2,1,0:T(8,128)S(1)}, f32[1,256,512]{2,1,0:T(8,128)S(1)}, u32[]{:S(2)}, u32[]{:S(2)}) %collective-permute-start.5) | collective-permute-done | bytes 524320 | tf_op jit(solution)/shard_map/cond/branch_0_fun/ppermute | solution.py:29
  (304 shorter events, 180.9 us)
Async XLA Ops:
  1.6 8.5 %collective-permute-start.8 = (bf16[320,1024]{1,0:T(8,128)(2,1)S(1)}, bf16[320,1024]{1,0:T(8,128)(2,1)S(1)}, u32[]{:S(2)}, u32[]{:S(2)}) collective-permute-start(bf16[320,1024]{1,0:T(8,128)(2,1)S(1)} %get-tuple-element.226.refs_0_), channel_id=1, source_target_pairs={{0,1},{1,0},{2,3},{3,2},{4,5},{5,4},{6,7},{7,6},{8,9},{9,8},{10,11... | collective-permute-start | bytes 1966088 | tf_op jit(solution)/shard_map/ppermute | solution.py:29
  2.1 17.9 %collective-permute-start.11 = (bf16[320,1024]{1,0:T(8,128)(2,1)S(1)}, bf16[320,1024]{1,0:T(8,128)(2,1)S(1)}, u32[]{:S(2)}, u32[]{:S(2)}) collective-permute-start(bf16[320,1024]{1,0:T(8,128)(2,1)S(1)} %get-tuple-element.226.refs_0_), channel_id=1, source_target_pairs={{0,2},{1,3},{2,0},{3,1},{4,6},{5,7},{6,4},{7,5},{8,10},{9,11},{10,... | collective-permute-start | bytes 1966088 | tf_op jit(solution)/shard_map/ppermute | solution.py:29
  4.7 5.4 collective-permute-start.9
  6.3 1.4 collective-permute-start.6
  7.7 11.0 %collective-permute-start.7 = (f32[264,128]{1,0:T(8,128)S(1)}, f32[264,128]{1,0:T(8,128)S(1)}, u32[]{:S(2)}, u32[]{:S(2)}) collective-permute-start(f32[264,128]{1,0:T(8,128)S(1)} %add.134), channel_id=1, source_target_pairs={{0,8},{4,12},{8,0},{12,4},{16,24},{20,28},{24,16},{28,20},{1,9},{5... | collective-permute-start | bytes 405512 | tf_op jit(solution)/shard_map/ppermute | solution.py:29
  10.1 14.3 %copy-start.4 = (s32[1,8]{1,0:T(1,128)S(1)}, s32[1,8]{1,0:T(1,128)}, u32[]{:S(2)}) copy-start(s32[1,8]{1,0:T(1,128)} %param.15) | copy-start | bytes 100
  10.1 14.3 %copy-start.5 = (s32[40]{0:T(128)S(1)}, s32[40]{0:T(128)}, u32[]{:S(2)}) copy-start(s32[40]{0:T(128)} %items.5) | copy-start | bytes 484
  10.1 14.3 %copy-start.6 = (s32[40]{0:T(128)S(1)}, s32[40]{0:T(128)}, u32[]{:S(2)}) copy-start(s32[40]{0:T(128)} %users.5) | copy-start | bytes 484
  20.0 4.4 collective-permute-start.12
  20.0 12.7 %collective-permute-start.16 = (bf16[192,1024]{1,0:T(8,128)(2,1)S(1)}, bf16[192,1024]{1,0:T(8,128)(2,1)S(1)}, u32[]{:S(2)}, u32[]{:S(2)}) collective-permute-start(bf16[192,1024]{1,0:T(8,128)(2,1)S(1)} %get-tuple-element.227.refs_1_), channel_id=1, source_target_pairs={{0,2},{1,3},{2,0},{3,1},{4,6},{5,7},{6,4},{7,5},{8,10},{9,11},{10,... | collective-permute-start | bytes 1179656 | tf_op jit(solution)/shard_map/ppermute | solution.py:29
  21.8 10.9 %collective-permute-start.10 = (f32[264,128]{1,0:T(8,128)S(1)}, f32[264,128]{1,0:T(8,128)S(1)}, u32[]{:S(2)}, u32[]{:S(2)}) collective-permute-start(f32[264,128]{1,0:T(8,128)S(1)} %add.135), channel_id=1, source_target_pairs={{0,16},{4,20},{8,24},{12,28},{16,0},{20,4},{24,8},{28,12},{1,17},{... | collective-permute-start | bytes 405512 | tf_op jit(solution)/shard_map/ppermute | solution.py:29
  32.8 3.6 collective-permute-start.17
  32.8 10.6 %collective-permute-start.14 = (bf16[640,256]{1,0:T(8,128)(2,1)S(1)}, bf16[640,256]{1,0:T(8,128)(2,1)S(1)}, u32[]{:S(2)}, u32[]{:S(2)}) collective-permute-start(bf16[640,256]{1,0:T(8,128)(2,1)S(1)} %bitcast.121), channel_id=1, source_target_pairs={{0,4},{4,0},{8,12},{12,8},{16,20},{20,16},{24,28},{28,24},{1,5},{5... | collective-permute-start | bytes 983048 | tf_op jit(solution)/shard_map/ppermute | solution.py:29
  33.3 10.2 %collective-permute-start.15 = (bf16[640,256]{1,0:T(8,128)(2,1)S(1)}, bf16[640,256]{1,0:T(8,128)(2,1)S(1)}, u32[]{:S(2)}, u32[]{:S(2)}) collective-permute-start(bf16[640,256]{1,0:T(8,128)(2,1)S(1)} %bitcast.120), channel_id=1, source_target_pairs={{0,8},{4,12},{8,0},{12,4},{16,24},{20,28},{24,16},{28,20},{1,9},{5... | collective-permute-start | bytes 983048 | tf_op jit(solution)/shard_map/ppermute | solution.py:29
  35.5 7.9 %collective-permute-start.13 = (f32[264,128]{1,0:T(8,128)S(1)}, f32[264,128]{1,0:T(8,128)S(1)}, u32[]{:S(2)}, u32[]{:S(2)}) collective-permute-start(f32[264,128]{1,0:T(8,128)S(1)} %add.136), channel_id=1, source_target_pairs={{0,2},{1,3},{2,0},{3,1},{4,6},{5,7},{6,4},{7,5},{8,10},{9,11},{10,... | collective-permute-start | bytes 405512 | tf_op jit(solution)/shard_map/ppermute | solution.py:29
  43.7 12.4 %collective-permute-start.19 = (bf16[704,256]{1,0:T(8,128)(2,1)S(1)}, bf16[704,256]{1,0:T(8,128)(2,1)S(1)}, u32[]{:S(2)}, u32[]{:S(2)}) collective-permute-start(bf16[704,256]{1,0:T(8,128)(2,1)S(1)} %pad_maximum_fusion.2), channel_id=1, source_target_pairs={{0,4},{4,0},{8,12},{12,8},{16,20},{20,16},{24,28},{28,24},{1,5},{5... | collective-permute-start | bytes 1081352 | tf_op jit(solution)/shard_map/ppermute | solution.py:29
  45.0 11.1 %collective-permute-start.20 = (bf16[704,256]{1,0:T(8,128)(2,1)S(1)}, bf16[704,256]{1,0:T(8,128)(2,1)S(1)}, u32[]{:S(2)}, u32[]{:S(2)}) collective-permute-start(bf16[704,256]{1,0:T(8,128)(2,1)S(1)} %pad_maximum_fusion.3), channel_id=1, source_target_pairs={{0,8},{4,12},{8,0},{12,4},{16,24},{20,28},{24,16},{28,20},{1,9},{5... | collective-permute-start | bytes 1081352 | tf_op jit(solution)/shard_map/ppermute | solution.py:29
  46.7 9.4 %collective-permute-start.18 = (f32[264,128]{1,0:T(8,128)S(1)}, f32[264,128]{1,0:T(8,128)S(1)}, u32[]{:S(2)}, u32[]{:S(2)}) collective-permute-start(f32[264,128]{1,0:T(8,128)S(1)} %add.137), channel_id=1, source_target_pairs={{0,4},{4,0},{8,12},{12,8},{16,20},{20,16},{24,28},{28,24},{1,5},{5... | collective-permute-start | bytes 405512 | tf_op jit(solution)/shard_map/ppermute | solution.py:29
  56.2 17.3 %copy-start.1 = (f32[1024,256]{1,0:T(8,128)S(1)}, f32[1024,256]{1,0:T(8,128)}, u32[]{:S(2)}) copy-start(f32[1024,256]{1,0:T(8,128)} %sketch.1) | copy-start | bytes 3145732
  56.4 9.6 %collective-permute-start.21 = (bf16[192,256]{1,0:T(8,128)(2,1)S(1)}, bf16[192,256]{1,0:T(8,128)(2,1)S(1)}, u32[]{:S(2)}, u32[]{:S(2)}) collective-permute-start(bf16[192,256]{1,0:T(8,128)(2,1)S(1)} %bitcast.131), channel_id=1, source_target_pairs={{0,4},{4,0},{8,12},{12,8},{16,20},{20,16},{24,28},{28,24},{1,5},{5... | collective-permute-start | bytes 294920 | tf_op jit(solution)/shard_map/ppermute | solution.py:29
  57.9 8.7 %collective-permute-start.23 = (bf16[320,256]{1,0:T(8,128)(2,1)S(1)}, bf16[320,256]{1,0:T(8,128)(2,1)S(1)}, u32[]{:S(2)}, u32[]{:S(2)}) collective-permute-start(bf16[320,256]{1,0:T(8,128)(2,1)S(1)} %pad_maximum_fusion.5), channel_id=1, source_target_pairs={{0,16},{4,20},{8,24},{12,28},{16,0},{20,4},{24,8},{28,12},{1,17},{... | collective-permute-start | bytes 491528 | tf_op jit(solution)/shard_map/ppermute | solution.py:29
  59.8 6.2 collective-permute-start.22
  66.8 6.7 %collective-permute-start.24 = (bf16[192,256]{1,0:T(8,128)(2,1)S(1)}, bf16[192,256]{1,0:T(8,128)(2,1)S(1)}, u32[]{:S(2)}, u32[]{:S(2)}) collective-permute-start(bf16[192,256]{1,0:T(8,128)(2,1)S(1)} %pad_maximum_fusion.6), channel_id=1, source_target_pairs={{0,16},{4,20},{8,24},{12,28},{16,0},{20,4},{24,8},{28,12},{1,17},{... | collective-permute-start | bytes 294920 | tf_op jit(solution)/shard_map/ppermute | solution.py:29
  136.4 13.0 %collective-permute-start.1 = (bf16[1024,256]{0,1:T(8,128)(2,1)S(1)}, bf16[1024,256]{0,1:T(8,128)(2,1)S(1)}, u32[]{:S(2)}, u32[]{:S(2)}) collective-permute-start(bf16[1024,256]{0,1:T(8,128)(2,1)S(1)} %pad_maximum_fusion.1), channel_id=1, source_target_pairs={{0,2},{1,3},{2,0},{3,1},{4,6},{5,7},{6,4},{7,5},{8,10},{9,11},{10,... | collective-permute-start | bytes 1572872 | tf_op jit(solution)/shard_map/cond/branch_0_fun/ppermute | solution.py:29
  137.3 12.1 %collective-permute-start = (bf16[1024,256]{0,1:T(8,128)(2,1)S(1)}, bf16[1024,256]{0,1:T(8,128)(2,1)S(1)}, u32[]{:S(2)}, u32[]{:S(2)}) collective-permute-start(bf16[1024,256]{0,1:T(8,128)(2,1)S(1)} %pad_maximum_fusion.1), channel_id=1, source_target_pairs={{0,1},{1,0},{2,3},{3,2},{4,5},{5,4},{6,7},{7,6},{8,9},{9,8},{10,11... | collective-permute-start | bytes 1572872 | tf_op jit(solution)/shard_map/cond/branch_0_fun/ppermute | solution.py:29
  149.4 2.0 collective-permute-start.2
  149.4 0.8 copy-start.3
  593.3 49.9 %copy-start = (f32[8,256,512]{2,1,0:T(8,128)S(1)}, f32[8,256,512]{2,1,0:T(8,128)}, u32[]{:S(2)}) copy-start(f32[8,256,512]{2,1,0:T(8,128)} %get-tuple-element.173) | copy-start | bytes 12582916 | tf_op jit(solution)/shard_map/cond
  595.3 47.9 %collective-permute-start.3 = (f32[4,256,512]{2,1,0:T(8,128)S(1)}, f32[4,256,512]{2,1,0:T(8,128)S(1)}, u32[]{:S(2)}, u32[]{:S(2)}) collective-permute-start(f32[4,256,512]{2,1,0:T(8,128)S(1)} %slice.118), channel_id=1, source_target_pairs={{0,16},{4,20},{8,24},{12,28},{16,0},{20,4},{24,8},{28,12},{1,17},{... | collective-permute-start | bytes 6291464 | tf_op jit(solution)/shard_map/cond/branch_0_fun/ppermute | solution.py:29
  643.8 14.9 %collective-permute-start.4 = (f32[2,256,512]{2,1,0:T(8,128)S(1)}, f32[2,256,512]{2,1,0:T(8,128)S(1)}, u32[]{:S(2)}, u32[]{:S(2)}) collective-permute-start(f32[2,256,512]{2,1,0:T(8,128)S(1)} %slice.178), channel_id=1, source_target_pairs={{0,8},{4,12},{8,0},{12,4},{16,24},{20,28},{24,16},{28,20},{1,9},{5... | collective-permute-start | bytes 3145736 | tf_op jit(solution)/shard_map/cond/branch_0_fun/ppermute | solution.py:29
  658.9 9.2 %collective-permute-start.5 = (f32[1,256,512]{2,1,0:T(8,128)S(1)}, f32[1,256,512]{2,1,0:T(8,128)S(1)}, u32[]{:S(2)}, u32[]{:S(2)}) collective-permute-start(f32[1,256,512]{2,1,0:T(8,128)S(1)} %slice.180), channel_id=1, source_target_pairs={{0,4},{4,0},{8,12},{12,8},{16,20},{20,16},{24,28},{28,24},{1,5},{5... | collective-permute-start | bytes 1572872 | tf_op jit(solution)/shard_map/cond/branch_0_fun/ppermute | solution.py:29
  668.5 0.8 copy-start.2
